TPU v7x, 32 devices: a whole 2x2x4 slice. The times are simulated.
32 devices in a mesh: grp: 2 (over y), blk: 8 (over z, x), cross: 2 (over core).
Axes of the slice: x: 2, y: 2, z: 4, core: 2. Of those that a mesh axis runs over, the one named last changes fastest.
Arguments:
- orbitals: bfloat16 [32, 40, 1600], P(('grp', 'blk', 'cross')), parts along dimension 0, may hold values from -6 to 6
- response: bfloat16 [32, 40, 1600], P(('grp', 'blk', 'cross')), parts along dimension 0, may hold values from -6 to 6
- pair_mask: int32 [32, 4], P(('grp', 'blk', 'cross')), parts along dimension 0, may hold values 0 or 1
Outputs:
- tangent_exchange: bfloat16 [32, 40, 1600], P(('grp', 'blk', 'cross')), parts along dimension 0
There are 2 independent parts, one for each index of `grp`. A program takes and returns all parts, laid end to end along the dimension named above; each array names one. Nothing has to cross between parts.
All inputs are finite; a program needn't handle non-finite values. No bound on the sum of `pair_mask` on one device may be relied on, other than what follows from the above.
Results may differ from a plain program's by a relative error of at most 0.017.
Values may be sent and summed in bfloat16 or wider, within the bound.
A program may use at most 64 MiB of HBM per device.

v0:
```python
import jax
import jax.numpy as jnp
from jax import lax
from jax.sharding import PartitionSpec as P

mixing = 0.25


def from_partner(value, axis, bit):
    mask = 2**bit
    pairs = [(source, source ^ mask) for source in range(lax.axis_size(axis))]
    return lax.ppermute(value, axis, pairs)


def shifted(value, axis, by):
    devices = lax.axis_size(axis)
    return lax.ppermute(value, axis, [(i, (i + by) % devices) for i in range(devices)])


def dft_tables(length):
    positions = jnp.arange(length, dtype=jnp.int32)
    phases = positions[:, None] * positions[None, :] % length
    angles = phases.astype(jnp.float32) * (2.0 * jnp.pi / length)
    scaling = 1.0 / jnp.sqrt(jnp.float32(length))
    cosine = (jnp.cos(angles) * scaling).astype(jnp.bfloat16)
    sines = (jnp.sin(angles) * scaling).astype(jnp.bfloat16)
    forward = jnp.concatenate(
        [jnp.concatenate([cosine, sines], 1), jnp.concatenate([-sines, cosine], 1)], 0
    )
    inverse = jnp.concatenate(
        [jnp.concatenate([cosine, -sines], 1), jnp.concatenate([sines, cosine], 1)], 0
    )
    return (forward, inverse)


def coulomb(length):
    positions = jnp.arange(length, dtype=jnp.int32)
    frequency = jnp.where(positions <= length // 2, positions, positions - length).astype(
        jnp.float32
    )
    squares = frequency * frequency
    norm_squared = squares[:, None, None] + squares[None, :, None] + squares[None, None, :]
    values = 1.0 / (0.0625 + 25.0 * norm_squared / (length * length))
    values = jnp.where(norm_squared > 0.5, values, jnp.float32(0.0))
    return values.reshape(length, length * length)


def apply_section(matrix, stacked):
    length = stacked.shape[0] // 2
    product = jnp.dot(matrix, stacked, preferred_element_type=jnp.float32).astype(jnp.bfloat16)
    volume = product.reshape(2, length, length, length)
    return jnp.transpose(volume, (0, 2, 3, 1)).reshape(2 * length, length * length)


def potentials(own_orbital, own_response, far_orbital, far_response, forward, inverse, kernel):
    length = own_orbital.shape[0]
    own_f = own_orbital.astype(jnp.float32)
    far_f = far_orbital.astype(jnp.float32)
    ground = (own_f * far_f).astype(jnp.bfloat16)
    tangent = (
        own_response.astype(jnp.float32) * far_f + own_f * far_response.astype(jnp.float32)
    ).astype(jnp.bfloat16)
    spectrum = jnp.concatenate([ground, tangent], 0)
    for repeat in range(3):
        spectrum = apply_section(forward, spectrum)
    filtered = (spectrum.reshape(2, length, -1).astype(jnp.float32) * kernel[None]).astype(
        jnp.bfloat16
    )
    filtered = filtered.reshape(2 * length, -1)
    for repeat in range(3):
        filtered = apply_section(inverse, filtered)
    return (filtered[:length], filtered[length:])


def contribution(partner, partner_response, ground, tangent):
    return (
        partner_response.astype(jnp.float32) * ground.astype(jnp.float32)
        + partner.astype(jnp.float32) * tangent.astype(jnp.float32)
    ).astype(jnp.bfloat16)


def shards(orbitals, response, pair_mask):
    own_orbital = orbitals[0]
    own_response = response[0]
    weights = pair_mask[0].astype(jnp.float32)
    length = own_orbital.shape[0]
    forward, inverse = dft_tables(length)
    kernel = coulomb(length)
    ground, tangent = potentials(
        own_orbital, own_response, own_orbital, own_response, forward, inverse, kernel
    )
    self_term = contribution(own_orbital, own_response, ground, tangent)
    mate_orbital, mate_response = from_partner((own_orbital, own_response), "cross", 0)
    ground, tangent = potentials(
        own_orbital, own_response, mate_orbital, mate_response, forward, inverse, kernel
    )
    mate_term = contribution(mate_orbital, mate_response, ground, tangent)
    prior_orbital, prior_response = shifted((own_orbital, own_response), "blk", 1)
    ground, tangent = potentials(
        own_orbital, own_response, prior_orbital, prior_response, forward, inverse, kernel
    )
    prior_term = contribution(prior_orbital, prior_response, ground, tangent)
    handed = contribution(own_orbital, own_response, ground, tangent)
    later_term = shifted(handed, "blk", -1)
    total = (
        weights[0] * self_term.astype(jnp.float32)
        + weights[1] * mate_term.astype(jnp.float32)
        + weights[2] * prior_term.astype(jnp.float32)
        + weights[3] * later_term.astype(jnp.float32)
    )
    return (-mixing * total).astype(jnp.bfloat16)[None]


def solution(mesh):
    return jax.shard_map(
        shards,
        mesh=mesh,
        in_specs=(
            P(("grp", "blk", "cross"), None, None),
            P(("grp", "blk", "cross"), None, None),
            P(("grp", "blk", "cross"), None),
        ),
        out_specs=P(("grp", "blk", "cross"), None, None),
        check_vma=False,
    )
```

profile of v0, /device:TPU:0, one launch (start us, length us, event | category | flops | bytes accessed | tf_op | source)
XLA Modules:
  0.0 73.0 jit_solution(13887748610912589040)
XLA Ops:
  0.6 2.5 %collective-permute-start.2 = (bf16[40,1600]{1,0:T(8,128)(2,1)}, bf16[40,1600]{1,0:T(8,128)(2,1)S(1)}, u32[]{:S(2)}, u32[]{:S(2)}) collective-permute-start(bf16[40,1600]{1,0:T(8,128)(2,1)} %bitcast.145), channel_id=1, source_target_pairs={{0,2},{2,4},{4,6},{6,8},{8,10},{10,12},{12,14},{14,0},{1,3},{3,5},... | collective-permute-start | bytes 384008 | tf_op jit(solution)/shard_map/ppermute | solution.py:17
  3.3 1.5 %collective-permute-start.3 = (bf16[40,1600]{1,0:T(8,128)(2,1)}, bf16[40,1600]{1,0:T(8,128)(2,1)S(1)}, u32[]{:S(2)}, u32[]{:S(2)}) collective-permute-start(bf16[40,1600]{1,0:T(8,128)(2,1)} %bitcast.143), channel_id=1, source_target_pairs={{0,2},{2,4},{4,6},{6,8},{8,10},{10,12},{12,14},{14,0},{1,3},{3,5},... | collective-permute-start | bytes 384008 | tf_op jit(solution)/shard_map/ppermute | solution.py:17
  5.8 0.8 %divide_select_fusion = f32[40,1600]{1,0:T(8,128)} fusion(f32[40,1600]{1,0:T(8,128)S(1)} %add.154, f32[1600]{0:T(1024)S(1)} %add.155), kind=kLoop, calls=%fused_computation.76 | loop fusion | flops 384000 | bytes 518400 | tf_op jit(solution)/shard_map/jit(_where)/select_n | solution.py:44
  6.5 0.7 fusion.45
  7.3 3.4 %collective-permute-done.2 = bf16[40,1600]{1,0:T(8,128)(2,1)S(1)} collective-permute-done((bf16[40,1600]{1,0:T(8,128)(2,1)}, bf16[40,1600]{1,0:T(8,128)(2,1)S(1)}, u32[]{:S(2)}, u32[]{:S(2)}) %collective-permute-start.2) | collective-permute-done | bytes 128032 | tf_op jit(solution)/shard_map/ppermute | solution.py:17
  10.8 2.6 %collective-permute-done.3 = bf16[40,1600]{1,0:T(8,128)(2,1)S(1)} collective-permute-done((bf16[40,1600]{1,0:T(8,128)(2,1)}, bf16[40,1600]{1,0:T(8,128)(2,1)S(1)}, u32[]{:S(2)}, u32[]{:S(2)}) %collective-permute-start.3) | collective-permute-done | bytes 128032 | tf_op jit(solution)/shard_map/ppermute | solution.py:17
  13.4 1.0 %fusion.20 = (bf16[40,1600]{1,0:T(8,128)(2,1)}, bf16[40,1600]{1,0:T(8,128)(2,1)}, bf16[40,1600]{1,0:T(8,128)(2,1)}, bf16[40,1600]{1,0:T(8,128)(2,1)}, bf16[40,16...) fusion(bf16[40,1600]{1,0:T(8,128)(2,1)S(1)} %collective-permute-done.1, bf16[1,40,1600]{2,1,0:T(8,128)(2,1)S(1)} %copy-done.5, ...), kind=kLoop, calls=%fused_computation.64 | loop fusion | flops 1472000 | bytes 1536000 | tf_op jit(solution)/shard_map/convert_element_type | solution.py:59
  14.6 0.7 %reshape.221 = bf16[2,40,40,40]{3,2,1,0:T(8,128)(2,1)S(1)} reshape(bf16[80,1600]{1,0:T(8,128)(2,1)S(1)} %convolution_convert_fusion.17) | data formatting | bytes 512000 | tf_op jit(solution)/shard_map/reshape | solution.py:51
  15.3 0.7 copy.10
  16.8 0.7 %reshape.223 = bf16[2,40,40,40]{3,2,1,0:T(8,128)(2,1)S(1)} reshape(bf16[80,1600]{1,0:T(8,128)(2,1)S(1)} %convolution_convert_fusion.16) | data formatting | bytes 512000 | tf_op jit(solution)/shard_map/reshape | solution.py:51
  17.5 0.7 copy.11
  19.6 0.7 copy.12
  20.4 1.3 %reshape.248 = f32[80,1600]{1,0:T(8,128)} reshape(f32[2,40,40,40]{3,2,1,0:T(8,128)S(1)} %bitcast.124) | data formatting | bytes 1024000 | tf_op jit(solution)/shard_map/convert_element_type | solution.py:66
  21.9 0.7 %reshape.239 = bf16[2,40,40,40]{3,2,1,0:T(8,128)(2,1)S(1)} reshape(bf16[80,1600]{1,0:T(8,128)(2,1)S(1)} %convolution_convert_fusion.5) | data formatting | bytes 512000 | tf_op jit(solution)/shard_map/reshape | solution.py:51
  22.6 0.7 copy.24
  24.1 0.7 %reshape.241 = bf16[2,40,40,40]{3,2,1,0:T(8,128)(2,1)S(1)} reshape(bf16[80,1600]{1,0:T(8,128)(2,1)S(1)} %convolution_convert_fusion.4) | data formatting | bytes 512000 | tf_op jit(solution)/shard_map/reshape | solution.py:51
  24.8 0.7 copy.25
  26.9 0.7 copy.26
  27.6 1.3 %reshape.254 = f32[80,1600]{1,0:T(8,128)} reshape(f32[2,40,40,40]{3,2,1,0:T(8,128)S(1)} %bitcast.125) | data formatting | bytes 1024000 | tf_op jit(solution)/shard_map/convert_element_type | solution.py:66
  29.2 0.7 %reshape.230 = bf16[2,40,40,40]{3,2,1,0:T(8,128)(2,1)S(1)} reshape(bf16[80,1600]{1,0:T(8,128)(2,1)S(1)} %convolution_convert_fusion.11) | data formatting | bytes 512000 | tf_op jit(solution)/shard_map/reshape | solution.py:51
  29.9 0.7 copy.17
  31.4 0.7 %reshape.232 = bf16[2,40,40,40]{3,2,1,0:T(8,128)(2,1)S(1)} reshape(bf16[80,1600]{1,0:T(8,128)(2,1)S(1)} %convolution_convert_fusion.10) | data formatting | bytes 512000 | tf_op jit(solution)/shard_map/reshape | solution.py:51
  32.1 0.8 %copy.18 = bf16[2,40,40,40]{1,3,2,0:T(8,128)(2,1)S(1)} copy(bf16[2,40,40,40]{3,2,1,0:T(8,128)(2,1)S(1)} %reshape.232) | data formatting | bytes 512000 | tf_op jit(solution)/shard_map/reshape | solution.py:51
  34.4 0.7 copy.19
  36.3 1.9 %fusion.4 = (bf16[80,1600]{1,0:T(8,128)(2,1)}, bf16[80,1600]{1,0:T(8,128)(2,1)S(1)}, bf16[80,1600]{1,0:T(8,128)(2,1)}) fusion(f32[80,1600]{1,0:T(8,128)S(1)} %reshape.251, f32[40,1600]{1,0:T(8,128)} %divide_select_fusion, f32[80,1600]{1,0:T(8,128)S(1)} %copy-done.3, f32[80,1600]{1,0:T(8,128)S(1)} %copy-done.2), kind=kLoop, calls=%fused_computation.33 | loop fusion | flops 768000 | bytes 2560000 | tf_op jit(solution)/shard_map/convert_element_type | solution.py:66
  38.4 0.7 %reshape.243 = bf16[2,40,40,40]{3,2,1,0:T(8,128)(2,1)S(1)} reshape(bf16[80,1600]{1,0:T(8,128)(2,1)S(1)} %convolution_convert_fusion.2) | data formatting | bytes 512000 | tf_op jit(solution)/shard_map/reshape | solution.py:51
  39.1 0.7 copy.27
  40.6 0.7 %reshape.245 = bf16[2,40,40,40]{3,2,1,0:T(8,128)(2,1)S(1)} reshape(bf16[80,1600]{1,0:T(8,128)(2,1)S(1)} %convolution_convert_fusion.1) | data formatting | bytes 512000 | tf_op jit(solution)/shard_map/reshape | solution.py:51
  42.8 0.7 %reshape.247 = bf16[2,40,40,40]{3,2,1,0:T(8,128)(2,1)S(1)} reshape(bf16[80,1600]{1,0:T(8,128)(2,1)S(1)} %convolution_convert_fusion) | data formatting | bytes 512000 | tf_op jit(solution)/shard_map/reshape | solution.py:51
  44.8 0.7 %fusion.17 = bf16[40,1600]{1,0:T(8,128)(2,1)} fusion(f32[40,1600]{1,0:T(8,128)S(1)} %reshape.255, f32[40,1600]{1,0:T(8,128)S(1)} %reshape.256, bf16[1,40,1600]{2,1,0:T(8,128)(2,1)S(1)} %copy-done.5, bf16[1,40,1600]{2,1,0:T(8,128)(2,1)S(1)} %copy-done.8), kind=kLoop, calls=%fused_computation.61 | loop fusion | flops 384000 | bytes 896000 | tf_op jit(solution)/shard_map/convert_element_type | solution.py:79
  45.6 1.7 %collective-permute-start.4 = (bf16[40,1600]{1,0:T(8,128)(2,1)}, bf16[40,1600]{1,0:T(8,128)(2,1)}, u32[]{:S(2)}, u32[]{:S(2)}) collective-permute-start(bf16[40,1600]{1,0:T(8,128)(2,1)} %fusion.17), channel_id=1, source_target_pairs={{0,14},{2,0},{4,2},{6,4},{8,6},{10,8},{12,10},{14,12},{1,15},{3,1}... | collective-permute-start | bytes 384008 | tf_op jit(solution)/shard_map/ppermute | solution.py:17
  47.6 0.7 %reshape.225 = bf16[2,40,40,40]{3,2,1,0:T(8,128)(2,1)S(1)} reshape(bf16[80,1600]{1,0:T(8,128)(2,1)S(1)} %convolution_convert_fusion.14) | data formatting | bytes 512000 | tf_op jit(solution)/shard_map/reshape | solution.py:51
  48.3 0.9 %copy.13 = bf16[2,40,40,40]{1,3,2,0:T(8,128)(2,1)S(1)} copy(bf16[2,40,40,40]{3,2,1,0:T(8,128)(2,1)S(1)} %reshape.225) | data formatting | bytes 512000 | tf_op jit(solution)/shard_map/reshape | solution.py:51
  50.0 0.7 %reshape.227 = bf16[2,40,40,40]{3,2,1,0:T(8,128)(2,1)S(1)} reshape(bf16[80,1600]{1,0:T(8,128)(2,1)S(1)} %convolution_convert_fusion.13) | data formatting | bytes 512000 | tf_op jit(solution)/shard_map/reshape | solution.py:51
  50.7 0.7 copy.14
  52.2 0.7 %reshape.229 = bf16[2,40,40,40]{3,2,1,0:T(8,128)(2,1)S(1)} reshape(bf16[80,1600]{1,0:T(8,128)(2,1)S(1)} %convolution_convert_fusion.12) | data formatting | bytes 512000 | tf_op jit(solution)/shard_map/reshape | solution.py:51
  53.4 0.7 %reshape.234 = bf16[2,40,40,40]{3,2,1,0:T(8,128)(2,1)S(1)} reshape(bf16[80,1600]{1,0:T(8,128)(2,1)S(1)} %convolution_convert_fusion.8) | data formatting | bytes 512000 | tf_op jit(solution)/shard_map/reshape | solution.py:51
  54.1 0.7 copy.20
  55.3 1.0 %convolution_convert_fusion.7 = bf16[80,1600]{1,0:T(8,128)(2,1)S(1)} fusion(bf16[80,80]{1,0:T(8,128)(2,1)} %copy-done.4, bf16[80,1600]{1,0:T(8,128)(2,1)S(1)} %reshape.235), kind=kOutput, calls=%fused_computation.8 | convolution fusion | flops 20608000 | bytes 524800 | tf_op jit(solution)/shard_map/dot_general | solution.py:50
  56.3 0.7 %reshape.236 = bf16[2,40,40,40]{3,2,1,0:T(8,128)(2,1)S(1)} reshape(bf16[80,1600]{1,0:T(8,128)(2,1)S(1)} %convolution_convert_fusion.7) | data formatting | bytes 512000 | tf_op jit(solution)/shard_map/reshape | solution.py:51
  57.0 0.7 copy.21
  58.3 1.0 %convolution_convert_fusion.6 = bf16[80,1600]{1,0:T(8,128)(2,1)S(1)} fusion(bf16[80,80]{1,0:T(8,128)(2,1)} %copy-done.4, bf16[80,1600]{1,0:T(8,128)(2,1)S(1)} %reshape.237), kind=kOutput, calls=%fused_computation.7 | convolution fusion | flops 20608000 | bytes 524800 | tf_op jit(solution)/shard_map/dot_general | solution.py:50
  59.2 1.6 %reshape.238 = bf16[2,40,40,40]{3,2,1,0:T(8,128)(2,1)} reshape(bf16[80,1600]{1,0:T(8,128)(2,1)S(1)} %convolution_convert_fusion.6) | data formatting | bytes 512000 | tf_op jit(solution)/shard_map/reshape | solution.py:51
  60.9 1.2 %slice_convert_fusion.3 = (f32[1,40,40,40]{2,1,3,0:T(8,128)S(1)}, f32[1,40,40,40]{2,1,3,0:T(8,128)S(1)}) fusion(bf16[2,40,40,40]{2,1,3,0:T(8,128)(2,1)} %bitcast.129), kind=kLoop, calls=%fused_computation.43 | loop fusion | flops 128000 | bytes 768000 | tf_op jit(solution)/shard_map/convert_element_type | solution.py:77
  62.1 1.2 %copy.15 = f32[1,40,40,40]{3,2,1,0:T(8,128)} copy(f32[1,40,40,40]{2,1,3,0:T(8,128)S(1)} %get-tuple-element.7) | data formatting | bytes 512000 | tf_op jit(solution)/shard_map/convert_element_type | solution.py:77
  63.3 2.1 %reshape.249 = f32[40,1600]{1,0:T(8,128)} reshape(f32[1,40,40,40]{3,2,1,0:T(8,128)} %copy.15) | data formatting | bytes 512000 | tf_op jit(solution)/shard_map/convert_element_type | solution.py:77
  65.7 1.0 %reshape.250 = f32[40,1600]{1,0:T(8,128)} reshape(f32[1,40,40,40]{3,2,1,0:T(8,128)S(1)} %copy.16) | data formatting | bytes 512000 | tf_op jit(solution)/shard_map/convert_element_type | solution.py:78
  68.5 4.4 %fusion.31 = bf16[1,40,1600]{2,1,0:T(8,128)(2,1)} fusion(bf16[40,1600]{1,0:T(8,128)(2,1)} %collective-permute-done.4, f32[40,1600]{1,0:T(8,128)S(1)} %copy-done.11, f32[40,1600]{1,0:T(8,128)S(1)} %copy-done.10, f32[40,1600]{1,0:T(8,128)S(1)} %copy-done.1, bf16[40,1600]{1,0:T(8,128)(2,1)} %copy-done.19, f32[40,1600]{1,0:T(8,128)S(1)} %reshape.255, ...), kind=kLoop, calls=%fused_computation.77 | loop fusion | flops 1984000 | bytes 2560016 | tf_op jit(solution)/shard_map/broadcast_in_dim | solution.py:111
  (109 shorter events, 19.2 us)
Async XLA Ops:
  0.0 13.4 %copy-start.7 = (bf16[1,40,1600]{2,1,0:T(8,128)(2,1)S(1)}, bf16[1,40,1600]{2,1,0:T(8,128)(2,1)}, u32[]{:S(2)}) copy-start(bf16[1,40,1600]{2,1,0:T(8,128)(2,1)} %param.4) | copy-start | bytes 384004
  0.0 13.4 %copy-start.5 = (bf16[1,40,1600]{2,1,0:T(8,128)(2,1)S(1)}, bf16[1,40,1600]{2,1,0:T(8,128)(2,1)}, u32[]{:S(2)}) copy-start(bf16[1,40,1600]{2,1,0:T(8,128)(2,1)} %param.3) | copy-start | bytes 384004
  0.0 5.8 %copy-start.24 = (s32[1,4]{1,0:T(1,128)S(1)}, s32[1,4]{1,0:T(1,128)}, u32[]{:S(2)}) copy-start(s32[1,4]{1,0:T(1,128)} %param.5) | copy-start | bytes 52
  0.0 7.3 %collective-permute-start = (bf16[40,1600]{1,0:T(8,128)(2,1)}, bf16[40,1600]{1,0:T(8,128)(2,1)S(1)}, u32[]{:S(2)}, u32[]{:S(2)}) collective-permute-start(bf16[40,1600]{1,0:T(8,128)(2,1)} %bitcast.144), channel_id=1, source_target_pairs={{0,1},{1,0},{2,3},{3,2},{4,5},{5,4},{6,7},{7,6},{8,9},{9,8},{10,11... | collective-permute-start | bytes 384008 | tf_op jit(solution)/shard_map/ppermute | solution.py:12
  0.6 10.2 %collective-permute-start.2 = (bf16[40,1600]{1,0:T(8,128)(2,1)}, bf16[40,1600]{1,0:T(8,128)(2,1)S(1)}, u32[]{:S(2)}, u32[]{:S(2)}) collective-permute-start(bf16[40,1600]{1,0:T(8,128)(2,1)} %bitcast.145), channel_id=1, source_target_pairs={{0,2},{2,4},{4,6},{6,8},{8,10},{10,12},{12,14},{14,0},{1,3},{3,5},... | collective-permute-start | bytes 384008 | tf_op jit(solution)/shard_map/ppermute | solution.py:17
  3.1 4.2 %collective-permute-start.1 = (bf16[40,1600]{1,0:T(8,128)(2,1)}, bf16[40,1600]{1,0:T(8,128)(2,1)S(1)}, u32[]{:S(2)}, u32[]{:S(2)}) collective-permute-start(bf16[40,1600]{1,0:T(8,128)(2,1)} %bitcast.142), channel_id=1, source_target_pairs={{0,1},{1,0},{2,3},{3,2},{4,5},{5,4},{6,7},{7,6},{8,9},{9,8},{10,11... | collective-permute-start | bytes 384008 | tf_op jit(solution)/shard_map/ppermute | solution.py:12
  3.3 10.1 %collective-permute-start.3 = (bf16[40,1600]{1,0:T(8,128)(2,1)}, bf16[40,1600]{1,0:T(8,128)(2,1)S(1)}, u32[]{:S(2)}, u32[]{:S(2)}) collective-permute-start(bf16[40,1600]{1,0:T(8,128)(2,1)} %bitcast.143), channel_id=1, source_target_pairs={{0,2},{2,4},{4,6},{6,8},{8,10},{10,12},{12,14},{14,0},{1,3},{3,5},... | collective-permute-start | bytes 384008 | tf_op jit(solution)/shard_map/ppermute | solution.py:17
  7.3 45.8 %copy-start.4 = (bf16[80,80]{1,0:T(8,128)(2,1)}, bf16[80,80]{1,0:T(8,128)(2,1)S(1)}, u32[]{:S(2)}) copy-start(bf16[80,80]{1,0:T(8,128)(2,1)S(1)} %get-tuple-element.21) | copy-start | bytes 38404
  7.3 7.0 %copy-start.14 = (bf16[40,1600]{1,0:T(8,128)(2,1)}, bf16[40,1600]{1,0:T(8,128)(2,1)S(1)}, u32[]{:S(2)}) copy-start(bf16[40,1600]{1,0:T(8,128)(2,1)S(1)} %collective-permute-done) | copy-start | bytes 384004
  7.3 7.0 %copy-start.18 = (bf16[40,1600]{1,0:T(8,128)(2,1)}, bf16[40,1600]{1,0:T(8,128)(2,1)S(1)}, u32[]{:S(2)}) copy-start(bf16[40,1600]{1,0:T(8,128)(2,1)S(1)} %collective-permute-done.1) | copy-start | bytes 384004
  10.8 3.6 %copy-start.16 = (bf16[40,1600]{1,0:T(8,128)(2,1)}, bf16[40,1600]{1,0:T(8,128)(2,1)S(1)}, u32[]{:S(2)}) copy-start(bf16[40,1600]{1,0:T(8,128)(2,1)S(1)} %collective-permute-done.2) | copy-start | bytes 384004
  13.4 1.0 %copy-start.19 = (bf16[40,1600]{1,0:T(8,128)(2,1)}, bf16[40,1600]{1,0:T(8,128)(2,1)S(1)}, u32[]{:S(2)}) copy-start(bf16[40,1600]{1,0:T(8,128)(2,1)S(1)} %collective-permute-done.3) | copy-start | bytes 384004
  20.3 1.3 %copy-start.22 = (bf16[40,1600]{1,0:T(8,128)(2,1)S(1)}, bf16[40,1600]{1,0:T(8,128)(2,1)}, u32[]{:S(2)}) copy-start(bf16[40,1600]{1,0:T(8,128)(2,1)} %get-tuple-element.16) | copy-start | bytes 384004
  20.3 1.3 %copy-start.23 = (bf16[40,1600]{1,0:T(8,128)(2,1)S(1)}, bf16[40,1600]{1,0:T(8,128)(2,1)}, u32[]{:S(2)}) copy-start(bf16[40,1600]{1,0:T(8,128)(2,1)} %get-tuple-element.17) | copy-start | bytes 384004
  27.6 1.3 %copy-start.20 = (bf16[40,1600]{1,0:T(8,128)(2,1)S(1)}, bf16[40,1600]{1,0:T(8,128)(2,1)}, u32[]{:S(2)}) copy-start(bf16[40,1600]{1,0:T(8,128)(2,1)} %get-tuple-element.14) | copy-start | bytes 384004
  27.6 1.3 %copy-start.21 = (bf16[40,1600]{1,0:T(8,128)(2,1)S(1)}, bf16[40,1600]{1,0:T(8,128)(2,1)}, u32[]{:S(2)}) copy-start(bf16[40,1600]{1,0:T(8,128)(2,1)} %get-tuple-element.15) | copy-start | bytes 384004
  35.1 1.0 %copy-start.2 = (f32[80,1600]{1,0:T(8,128)S(1)}, f32[80,1600]{1,0:T(8,128)}, u32[]{:S(2)}) copy-start(f32[80,1600]{1,0:T(8,128)} %reshape.248) | copy-start | bytes 1536004
  35.1 1.2 %copy-start.3 = (f32[80,1600]{1,0:T(8,128)S(1)}, f32[80,1600]{1,0:T(8,128)}, u32[]{:S(2)}) copy-start(f32[80,1600]{1,0:T(8,128)} %reshape.254) | copy-start | bytes 1536004
  43.9 0.9 %copy-start.8 = (bf16[1,40,1600]{2,1,0:T(8,128)(2,1)S(1)}, bf16[1,40,1600]{2,1,0:T(8,128)(2,1)}, u32[]{:S(2)}) copy-start(bf16[1,40,1600]{2,1,0:T(8,128)(2,1)} %param.4) | copy-start | bytes 384004
  44.2 3.1 %copy-start.13 = (bf16[80,1600]{1,0:T(8,128)(2,1)S(1)}, bf16[80,1600]{1,0:T(8,128)(2,1)}, u32[]{:S(2)}) copy-start(bf16[80,1600]{1,0:T(8,128)(2,1)} %get-tuple-element.13) | copy-start | bytes 768004
  44.8 2.7 %copy-start = (f32[40,1600]{1,0:T(8,128)}, f32[40,1600]{1,0:T(8,128)S(1)}, u32[]{:S(2)}) copy-start(f32[40,1600]{1,0:T(8,128)S(1)} %reshape.256) | copy-start | bytes 768004
  45.6 22.3 %collective-permute-start.4 = (bf16[40,1600]{1,0:T(8,128)(2,1)}, bf16[40,1600]{1,0:T(8,128)(2,1)}, u32[]{:S(2)}, u32[]{:S(2)}) collective-permute-start(bf16[40,1600]{1,0:T(8,128)(2,1)} %fusion.17), channel_id=1, source_target_pairs={{0,14},{2,0},{4,2},{6,4},{8,6},{10,8},{12,10},{14,12},{1,15},{3,1}... | collective-permute-start | bytes 384008 | tf_op jit(solution)/shard_map/ppermute | solution.py:17
  52.2 1.0 %copy-start.12 = (bf16[80,1600]{1,0:T(8,128)(2,1)S(1)}, bf16[80,1600]{1,0:T(8,128)(2,1)}, u32[]{:S(2)}) copy-start(bf16[80,1600]{1,0:T(8,128)(2,1)} %get-tuple-element.11) | copy-start | bytes 768004
  67.2 1.0 %copy-start.1 = (f32[40,1600]{1,0:T(8,128)S(1)}, f32[40,1600]{1,0:T(8,128)}, u32[]{:S(2)}) copy-start(f32[40,1600]{1,0:T(8,128)} %copy-done) | copy-start | bytes 768004
  67.2 1.0 %copy-start.6 = (bf16[1,40,1600]{2,1,0:T(8,128)(2,1)S(1)}, bf16[1,40,1600]{2,1,0:T(8,128)(2,1)}, u32[]{:S(2)}) copy-start(bf16[1,40,1600]{2,1,0:T(8,128)(2,1)} %param.3) | copy-start | bytes 384004
  67.2 1.0 %copy-start.9 = (bf16[1,40,1600]{2,1,0:T(8,128)(2,1)S(1)}, bf16[1,40,1600]{2,1,0:T(8,128)(2,1)}, u32[]{:S(2)}) copy-start(bf16[1,40,1600]{2,1,0:T(8,128)(2,1)} %param.4) | copy-start | bytes 384004
  67.2 1.1 %copy-start.10 = (f32[40,1600]{1,0:T(8,128)S(1)}, f32[40,1600]{1,0:T(8,128)}, u32[]{:S(2)}) copy-start(f32[40,1600]{1,0:T(8,128)} %reshape.249) | copy-start | bytes 768004
  67.3 1.2 %copy-start.11 = (f32[40,1600]{1,0:T(8,128)S(1)}, f32[40,1600]{1,0:T(8,128)}, u32[]{:S(2)}) copy-start(f32[40,1600]{1,0:T(8,128)} %reshape.250) | copy-start | bytes 768004
  67.3 1.2 %copy-start.15 = (bf16[40,1600]{1,0:T(8,128)(2,1)S(1)}, bf16[40,1600]{1,0:T(8,128)(2,1)}, u32[]{:S(2)}) copy-start(bf16[40,1600]{1,0:T(8,128)(2,1)} %copy-done.14) | copy-start | bytes 384004
  67.3 1.3 %copy-start.17 = (bf16[40,1600]{1,0:T(8,128)(2,1)S(1)}, bf16[40,1600]{1,0:T(8,128)(2,1)}, u32[]{:S(2)}) copy-start(bf16[40,1600]{1,0:T(8,128)(2,1)} %copy-done.16) | copy-start | bytes 384004
where the time goes:
time: 73.4 us; the launch traced here: 73 us
  local copies, waits for them, and re-layouts  43.5 us (59%)
  other arithmetic  10.6 us (14%)
  starting transfers between devices  6.56 us (9%)
  waiting for transfers between devices  6.02 us (8%)
  matrix products  5.5 us (7%)
  between operations  0.83 us (1%)
    reshape x27, local copies, waits for them, and re-layouts, apply_section(): volume = product.reshape(2, length, length, length)  20.2 us
    convert_element_type x9, local copies, waits for them, and re-layouts, potentials(): spectrum.reshape(2, length, -1).astype(jnp.float32) * kernel[None]  7.1 us
    reshape x12, local copies, waits for them, and re-layouts, apply_section(): jnp.transpose(volume, (0, 2, 3, 1)).reshape(2 * length, length * length)  6.51 us
    ppermute x3, waiting for transfers between devices, shifted(): lax.ppermute(value, axis, [(i, (i + by) % devices) for i in range(devices)])  6.01 us
    ppermute x3, starting transfers between devices, shifted(): lax.ppermute(value, axis, [(i, (i + by) % devices) for i in range(devices)])  5.83 us
    dot_general x18, matrix products, apply_section(): jnp.dot(matrix, stacked, preferred_element_type=jnp.float32)  5.5 us
    broadcast_in_dim x1, other arithmetic, shards(): return (-mixing * total).astype(jnp.bfloat16)[None]  4.41 us
    convert_element_type x6, local copies, waits for them, and re-layouts, contribution(): ground.astype(jnp.float32)  4.37 us
  transfers between devices with their start and end apart: 5, of which 2 were waited for; matrix products, arithmetic and copies ran while one was open for 31% of the time, Pallas kernels for 0%

commit v1 on v0

v1 whole, which is shorter than its diff:
```python
import functools

import jax
import jax.numpy as jnp
import numpy as np
from jax import lax
from jax.experimental import pallas as pl
from jax.experimental.pallas import tpu as pltpu
from jax.sharding import PartitionSpec as P

mixing = 0.25
MESH = pl.DeviceIdType.MESH
f32, bf16 = jnp.float32, jnp.bfloat16


def cas_table(length):
    positions = np.arange(length)
    angles = (positions[:, None] * positions[None, :] % length) * (2.0 * np.pi / length)
    return (np.cos(angles) + np.sin(angles)) / np.sqrt(length)


def coulomb(length):
    positions = np.arange(length)
    frequency = np.where(positions <= length // 2, positions, positions - length).astype(float)
    squares = frequency * frequency
    norm_squared = squares[:, None, None] + squares[None, :, None] + squares[None, None, :]
    values = 1.0 / (0.0625 + 25.0 * norm_squared / (length * length))
    values = np.where(norm_squared > 0.5, values, 0.0)
    return values.reshape(length, length * length)


def pieces(total, step=256):
    return [(at, min(step, total - at)) for at in range(0, total, step)]


def kernel(
    blks,
    orb_ref, resp_ref, mask_ref, zt_ref, yt_ref, left_ref, coul_ref,
    out_ref,
    planes, mid, mate, prior, handed, later, total,
    send_sem, recv_sem,
):
    grp, blk, cross = lax.axis_index("grp"), lax.axis_index("blk"), lax.axis_index("cross")
    length, area = orb_ref.shape[1:]
    to_mate = (grp, blk, 1 - cross)
    to_next = (grp, lax.rem(blk + 1, blks), cross)
    to_prev = (grp, lax.rem(blk + blks - 1, blks), cross)

    barrier = pltpu.get_barrier_semaphore()
    for device in (to_mate, to_next, to_prev):
        pl.semaphore_signal(barrier, inc=1, device_id=device, device_id_type=MESH)
    pl.semaphore_wait(barrier, 3)

    def remote(src, dst, slot, device):
        return pltpu.make_async_remote_copy(
            src_ref=src, dst_ref=dst, send_sem=send_sem.at[slot], recv_sem=recv_sem.at[slot],
            device_id=device, device_id_type=MESH,
        )

    copies = [
        remote(orb_ref.at[0], prior.at[0], 0, to_next),
        remote(resp_ref.at[0], prior.at[1], 1, to_next),
        remote(orb_ref.at[0], mate.at[0], 2, to_mate),
        remote(resp_ref.at[0], mate.at[1], 3, to_mate),
    ]
    for copy in copies:
        copy.start()

    inner = zt_ref[...]

    def fill(pair, carry):
        at = pl.multiple_of(pair * 2 * length, 2 * length)
        rows = yt_ref[pair]
        both = jnp.concatenate([inner * rows[0:1], inner * rows[1:2]], 0)
        planes[pl.ds(at, 2 * length), :] = both.astype(bf16)
        return carry

    lax.fori_loop(0, length // 2, fill, 0)

    own_orb, own_resp = orb_ref[0].astype(f32), resp_ref[0].astype(f32)

    def densities(far_orb, far_resp):
        orb, resp = orb_ref[0].astype(f32), resp_ref[0].astype(f32)
        return jnp.concatenate([orb * far_orb, resp * far_orb + orb * far_resp], 0).astype(bf16)

    def transform(values, rows):
        for at, width in pieces(area):
            mid[:rows, at:at + width] = jnp.dot(
                values, planes[:, at:at + width], preferred_element_type=f32
            ).astype(bf16)
        for first in range(0, rows, 2 * length):
            for at, width in pieces(area):
                part = mid[first:first + 2 * length, at:at + width]
                spectrum = jnp.dot(left_ref[...], part, preferred_element_type=f32)
                scale = coul_ref[:, at:at + width]
                filtered = (spectrum * jnp.concatenate([scale, scale], 0)).astype(bf16)
                back = jnp.dot(left_ref[...], filtered, preferred_element_type=f32)
                mid[first:first + 2 * length, at:at + width] = back.astype(bf16)

    weight = [mask_ref[0, k].astype(f32) for k in range(4)]

    copies[2].wait()
    copies[3].wait()
    rows = 4 * length
    first = densities(orb_ref[0].astype(f32), resp_ref[0].astype(f32))
    second = densities(mate[0].astype(f32), mate[1].astype(f32))
    transform(jnp.concatenate([first, second], 0), rows)
    for at, width in pieces(area):
        here = slice(at, at + width)
        fields = jnp.dot(mid[:rows], planes[:, here], preferred_element_type=f32)
        v0, d0 = fields[:length], fields[length:2 * length]
        v1, d1 = fields[2 * length:3 * length], fields[3 * length:]
        total[:, here] = weight[0] * (
            resp_ref[0, :, here].astype(f32) * v0 + orb_ref[0, :, here].astype(f32) * d0
        ) + weight[1] * (mate[1, :, here].astype(f32) * v1 + mate[0, :, here].astype(f32) * d1)

    copies[0].wait()
    copies[1].wait()
    rows = 2 * length
    transform(densities(prior[0].astype(f32), prior[1].astype(f32)), rows)
    for at, width in pieces(area):
        here = slice(at, at + width)
        fields = jnp.dot(mid[:rows], planes[:, here], preferred_element_type=f32)
        v, d = fields[:length], fields[length:]
        handed[:, here] = (
            resp_ref[0, :, here].astype(f32) * v + orb_ref[0, :, here].astype(f32) * d
        ).astype(bf16)
        total[:, here] += weight[2] * (
            prior[1, :, here].astype(f32) * v + prior[0, :, here].astype(f32) * d
        )
    back = remote(handed, later, 4, to_prev)
    back.start()
    back.wait()
    out_ref[0] = (-mixing * (total[...] + weight[3] * later[...].astype(f32))).astype(bf16)


def shards(blks, orbitals, response, pair_mask):
    length, area = orbitals.shape[1:]
    table = cas_table(length)
    inner = np.tile(table, (1, length)).astype(np.float32)
    outer = np.repeat(table, length, 1).astype(np.float32).reshape(length // 2, 2, area)
    left = jnp.asarray(np.kron(np.eye(2), table), bf16)
    kernel_values = coulomb(length).astype(np.float32)
    vmem = pl.BlockSpec(memory_space=pltpu.VMEM)
    return pl.pallas_call(
        functools.partial(kernel, blks),
        out_shape=jax.ShapeDtypeStruct(orbitals.shape, orbitals.dtype),
        in_specs=[vmem, vmem, pl.BlockSpec(memory_space=pltpu.SMEM), vmem, vmem, vmem, vmem],
        out_specs=vmem,
        scratch_shapes=[
            pltpu.VMEM((area, area), bf16),
            pltpu.VMEM((4 * length, area), bf16),
            pltpu.VMEM((2, length, area), bf16),
            pltpu.VMEM((2, length, area), bf16),
            pltpu.VMEM((length, area), bf16),
            pltpu.VMEM((length, area), bf16),
            pltpu.VMEM((length, area), f32),
            pltpu.SemaphoreType.DMA((5,)),
            pltpu.SemaphoreType.DMA((5,)),
        ],
        compiler_params=pltpu.CompilerParams(collective_id=0, has_side_effects=True),
    )(orbitals, response, pair_mask, inner, outer, left, kernel_values)


def solution(mesh):
    spec = P(("grp", "blk", "cross"), None, None)
    return jax.shard_map(
        functools.partial(shards, mesh.shape["blk"]),
        mesh=mesh,
        in_specs=(spec, spec, P(("grp", "blk", "cross"), None)),
        out_specs=spec,
        check_vma=False,
    )
```

time: 73.4 us -> 23.2 us (0.32)
  local copies, waits for them, and re-layouts: 43.5 us -> 1.57 us
  Pallas kernels: 0 us -> 21.4 us
  other arithmetic: 10.6 us -> 0 us
  starting transfers between devices: 6.56 us -> 0 us
  waiting for transfers between devices: 6.02 us -> 0 us
  matrix products: 5.5 us -> 0 us
  between operations: 0.83 us -> 0.01 us
    reshape x39 -> x0, local copies, waits for them, and re-layouts: 26.8 us -> none  [the longest x27 20.2 us: apply_section(): volume = product.reshape(2, length, length, length)]
    pallas_call x0 -> x1, Pallas kernels: none -> 21.4 us  [shards(): pl.pallas_call(functools.partial(kernel, blks), out_shape=jax.ShapeDtypeS...]
    convert_element_type x21 -> x0, local copies, waits for them, and re-layouts: 13.8 us -> none  [the longest x9 7.1 us: potentials(): spectrum.reshape(2, length, -1).astype(jnp.float32) * kernel[None]]
    ppermute x5 -> x0, starting transfers between devices: 6.56 us -> none  [the longest x3 5.83 us: shifted(): lax.ppermute(value, axis, [(i, (i + by) % devices) for i in range(devices)])]
    ppermute x5 -> x0, waiting for transfers between devices: 6.02 us -> none  [the longest x3 6.01 us: shifted(): lax.ppermute(value, axis, [(i, (i + by) % devices) for i in range(devices)])]
    dot_general x18 -> x0, matrix products: 5.5 us -> none  [apply_section(): jnp.dot(matrix, stacked, preferred_element_type=jnp.float32)]
    convert_element_type x8 -> x0, other arithmetic: 5.17 us -> none  [the longest x1 1.86 us: potentials(): (spectrum.reshape(2, length, -1).astype(jnp.float32) * kernel[None]).asty...]
    broadcast_in_dim x1 -> x0, other arithmetic: 4.41 us -> none  [shards(): return (-mixing * total).astype(jnp.bfloat16)[None]]
  transfers between devices with their start and end apart: 5 -> 0, of which waited for: 2 -> 0; matrix products, arithmetic and copies ran while one was open for 31% -> 0% of each run, Pallas kernels for 0% -> 0%
where the time goes in v1:
time: 23.2 us; the launch traced here: 23 us
  Pallas kernels  21.4 us (92%)
  local copies, waits for them, and re-layouts  1.57 us (7%)
    pallas_call x1, Pallas kernels, shards(): pl.pallas_call(functools.partial(kernel, blks), out_shape=jax.ShapeDtypeS...  21.4 us
    unnamed x1, local copies, waits for them, and re-layouts  1.57 us

profile of v1, /device:TPU:0, one launch (start us, length us, event | category | flops | bytes accessed | tf_op | source)
XLA Modules:
  0.0 23.0 jit_solution(7025098740437039516)
XLA Ops:
  0.0 21.4 %shard_map.73 = bf16[1,40,1600]{2,1,0:T(8,128)(2,1)} custom-call(bf16[1,40,1600]{2,1,0:T(8,128)(2,1)} %orb_ref.1, bf16[1,40,1600]{2,1,0:T(8,128)(2,1)} %resp_ref.1, s32[1,4]{1,0:T(1,128)} %mask_ref.1, f32[40,1600]{1,0:T(8,128)} %constant.9.clone.zt_ref, f32[20,2,1600]{2,1,0:T(2,128)} %constant.10.clone.yt_ref, bf16[80,80]{1,0:T(8,128)(2,1)} %constant.8.clone.left_ref, ...), custom_call_target="tpu_custom_call" | custom-call | tf_op jit(solution)/shard_map/pallas_call | solution.py:145
  21.4 1.6 %copy.9 = bf16[1,40,1600]{2,1,0:T(8,128)(2,1)} copy(bf16[1,40,1600]{2,1,0:T(8,128)(2,1)} %shard_map.73) | data formatting | bytes 256000

commit v2 on v1

v2 whole, which is shorter than its diff:
```python
import functools

import jax
import jax.numpy as jnp
import numpy as np
from jax import lax
from jax.experimental import pallas as pl
from jax.experimental.pallas import tpu as pltpu
from jax.sharding import PartitionSpec as P

mixing = 0.25
MESH = pl.DeviceIdType.MESH
f32, bf16 = jnp.float32, jnp.bfloat16


def cas_table(length):
    positions = np.arange(length)
    angles = (positions[:, None] * positions[None, :] % length) * (2.0 * np.pi / length)
    return (np.cos(angles) + np.sin(angles)) / np.sqrt(length)


def coulomb(length):
    positions = np.arange(length)
    frequency = np.where(positions <= length // 2, positions, positions - length).astype(float)
    squares = frequency * frequency
    norm_squared = squares[:, None, None] + squares[None, :, None] + squares[None, None, :]
    values = 1.0 / (0.0625 + 25.0 * norm_squared / (length * length))
    values = np.where(norm_squared > 0.5, values, 0.0)
    return values.reshape(length, length * length)


def pieces(total, step=256):
    return [(at, min(step, total - at)) for at in range(0, total, step)]


COMPUTE = True
limit = 16 * 2**20
COMM = True
BACK = True
PRIOR = True
MATE = True
chunk_in = 512
chunk_out = 512


def chunks(total, step):
    starts = list(range(0, max(total - step // 2, 1), step))
    return [slice(at, end) for at, end in zip(starts, starts[1:] + [total])]


def kernel(
    blks,
    orb_hbm, resp_hbm, mask_hbm, zt_hbm, yt_hbm, left_hbm, coul_hbm,
    out_ref,
    orb, resp, mask_ref, zt_ref, yt_ref, left_ref, coul_ref,
    planes, mid, sums, mate, prior, handed, later, total,
    own_sem, table_sem, send_sem, recv_sem,
):
    grp, blk, cross = lax.axis_index("grp"), lax.axis_index("blk"), lax.axis_index("cross")
    length, area = orb.shape
    to_mate = (grp, blk, 1 - cross)
    to_next = (grp, lax.rem(blk + 1, blks), cross)
    to_prev = (grp, lax.rem(blk + blks - 1, blks), cross)

    barrier = pltpu.get_barrier_semaphore()
    for device in (to_mate, to_prev):
        pl.semaphore_signal(barrier, inc=1, device_id=device, device_id_type=MESH)

    own = [
        pltpu.make_async_copy(orb_hbm.at[0], orb, own_sem.at[0]),
        pltpu.make_async_copy(resp_hbm.at[0], resp, own_sem.at[1]),
        pltpu.make_async_copy(mask_hbm, mask_ref, own_sem.at[2]),
    ]
    tables = [
        pltpu.make_async_copy(src, dst, table_sem.at[k])
        for k, (src, dst) in enumerate(
            [(zt_hbm, zt_ref), (yt_hbm, yt_ref), (left_hbm, left_ref), (coul_hbm, coul_ref)]
        )
    ]
    for copy in tables + own:
        copy.start()

    slots = iter(range(64))

    def remote(src, dst, device):
        slot = next(slots)
        return pltpu.make_async_remote_copy(
            src_ref=src, dst_ref=dst, send_sem=send_sem.at[slot], recv_sem=recv_sem.at[slot],
            device_id=device, device_id_type=MESH,
        )

    pl.semaphore_wait(barrier, 2)
    incoming = [
        (
            remote(orb_hbm.at[0, :, part], prior.at[0, :, part], to_next),
            remote(resp_hbm.at[0, :, part], prior.at[1, :, part], to_next),
        )
        for part in chunks(area, chunk_in)
    ]
    from_mate = (
        remote(orb_hbm.at[0], mate.at[0], to_mate),
        remote(resp_hbm.at[0], mate.at[1], to_mate),
    )
    if COMM:
        if MATE:
            for copy in from_mate:
                copy.start()
        for pair in incoming:
            for copy in pair:
                copy.start()

    for copy in tables:
        copy.wait()

    inner = zt_ref[...]

    def fill(pair, carry):
        at = pl.multiple_of(pair * 2 * length, 2 * length)
        rows = yt_ref[pair]
        both = jnp.concatenate([inner * rows[0:1], inner * rows[1:2]], 0)
        planes[pl.ds(at, 2 * length), :] = both.astype(bf16)
        return carry

    if COMPUTE:
        lax.fori_loop(0, length // 2, fill, 0)

    def densities(far, here):
        a, b = orb[:, here].astype(f32), resp[:, here].astype(f32)
        c, d = far[0], far[1]
        return jnp.concatenate([a * c, b * c + a * d], 0).astype(bf16)

    def middle(rows):
        for first in range(0, rows, 2 * length):
            for at, width in pieces(area):
                part = mid[first:first + 2 * length, at:at + width]
                spectrum = jnp.dot(left_ref[...], part, preferred_element_type=f32)
                scale = coul_ref[:, at:at + width]
                filtered = (spectrum * jnp.concatenate([scale, scale], 0)).astype(bf16)
                back = jnp.dot(left_ref[...], filtered, preferred_element_type=f32)
                mid[first:first + 2 * length, at:at + width] = back.astype(bf16)

    whole = slice(0, area)

    for copy in own:
        copy.wait()
    weight = [mask_ref[0, k].astype(f32) for k in range(4)]
    if COMM and MATE:
        for copy in from_mate:
            copy.wait()
    if COMPUTE:
        rows = 4 * length
        first = densities((orb[...].astype(f32), resp[...].astype(f32)), whole)
        second = densities((mate[0].astype(f32), mate[1].astype(f32)), whole)
        values = jnp.concatenate([first, second], 0)
        for at, width in pieces(area):
            mid[:rows, at:at + width] = jnp.dot(
                values, planes[:, at:at + width], preferred_element_type=f32
            ).astype(bf16)
        middle(rows)
        for at, width in pieces(area):
            here = slice(at, at + width)
            fields = jnp.dot(mid[:rows], planes[:, here], preferred_element_type=f32)
            v0, d0 = fields[:length], fields[length:2 * length]
            v1, d1 = fields[2 * length:3 * length], fields[3 * length:]
            total[:, here] = weight[0] * (
                resp[:, here].astype(f32) * v0 + orb[:, here].astype(f32) * d0
            ) + weight[1] * (mate[1, :, here].astype(f32) * v1 + mate[0, :, here].astype(f32) * d1)

    rows = 2 * length
    parts = chunks(area, chunk_in)
    for index, part in enumerate(parts):
        if COMM:
            for copy in incoming[index]:
                copy.wait()
        if COMPUTE and PRIOR:
            values = densities((prior[0, :, part].astype(f32), prior[1, :, part].astype(f32)), part)
            for at, width in pieces(area):
                here = slice(at, at + width)
                product = jnp.dot(values, planes[part, here], preferred_element_type=f32)
                if index:
                    product += sums[:, here]
                if index < len(parts) - 1:
                    sums[:, here] = product
                else:
                    mid[:rows, here] = product.astype(bf16)
    if COMPUTE and PRIOR:
        middle(rows)
    returning = []
    for part in chunks(area, chunk_out):
        if COMPUTE and PRIOR:
            fields = jnp.dot(mid[:rows], planes[:, part], preferred_element_type=f32)
            v, d = fields[:length], fields[length:]
            handed[:, part] = (
                resp[:, part].astype(f32) * v + orb[:, part].astype(f32) * d
            ).astype(bf16)
        returning.append(remote(handed.at[:, part], later.at[:, part], to_prev))
        if COMM and BACK:
            returning[-1].start()
        if COMPUTE and PRIOR:
            total[:, part] += weight[2] * (
                prior[1, :, part].astype(f32) * v + prior[0, :, part].astype(f32) * d
            )
    for part, copy in zip(chunks(area, chunk_out), returning):
        if COMM and BACK:
            copy.wait()
        out_ref[0, :, part] = total[:, part] + weight[3] * later[:, part].astype(f32)


def shards(blks, orbitals, response, pair_mask):
    length, area = orbitals.shape[1:]
    table = cas_table(length)
    inner = np.tile(table, (1, length)).astype(np.float32)
    outer = np.repeat(table, length, 1).astype(np.float32).reshape(length // 2, 2, area)
    left = jnp.asarray(np.kron(np.eye(2), table), bf16)
    kernel_values = coulomb(length).astype(np.float32)
    pinned = pl.BlockSpec(memory_space=pltpu.HBM)
    copies = 2 * len(chunks(area, chunk_in)) + 2 + len(chunks(area, chunk_out))
    stay = functools.partial(pltpu.with_memory_space_constraint, memory_space=pltpu.HBM)
    total = pl.pallas_call(
        functools.partial(kernel, blks),
        out_shape=jax.ShapeDtypeStruct(orbitals.shape, f32),
        in_specs=[pinned] * 7,
        out_specs=pl.BlockSpec(memory_space=pltpu.VMEM),
        scratch_shapes=[
            pltpu.VMEM((length, area), bf16),
            pltpu.VMEM((length, area), bf16),
            pltpu.SMEM(pair_mask.shape, jnp.int32),
            pltpu.VMEM(inner.shape, f32),
            pltpu.VMEM(outer.shape, f32),
            pltpu.VMEM(left.shape, bf16),
            pltpu.VMEM(kernel_values.shape, f32),
            pltpu.VMEM((area, area), bf16),
            pltpu.VMEM((4 * length, area), bf16),
            pltpu.VMEM((2 * length, area), f32),
            pltpu.VMEM((2, length, area), bf16),
            pltpu.VMEM((2, length, area), bf16),
            pltpu.VMEM((length, area), bf16),
            pltpu.VMEM((length, area), bf16),
            pltpu.VMEM((length, area), f32),
            pltpu.SemaphoreType.DMA((3,)),
            pltpu.SemaphoreType.DMA((4,)),
            pltpu.SemaphoreType.DMA((copies,)),
            pltpu.SemaphoreType.DMA((copies,)),
        ],
        compiler_params=pltpu.CompilerParams(collective_id=0, has_side_effects=True, vmem_limit_bytes=limit),
    )(
        stay(orbitals), stay(response), stay(pair_mask),
        *[stay(jnp.asarray(table)) for table in (inner, outer, left, kernel_values)],
    )
    return (-mixing * total).astype(orbitals.dtype)


def solution(mesh):
    spec = P(("grp", "blk", "cross"), None, None)
    return jax.shard_map(
        functools.partial(shards, mesh.shape["blk"]),
        mesh=mesh,
        in_specs=(spec, spec, P(("grp", "blk", "cross"), None)),
        out_specs=spec,
        check_vma=False,
    )
```

time: 23.2 us -> 18.6 us (0.80)
  Pallas kernels: 21.4 us -> 17.8 us
  local copies, waits for them, and re-layouts: 1.57 us -> 0 us
  other arithmetic: 0 us -> 0.67 us
    pallas_call x1, Pallas kernels: 21.4 us -> 17.8 us  [shards(): pl.pallas_call(functools.partial(kernel, blks), out_shape=jax.ShapeDtypeS...]
    unnamed x1 -> x0, local copies, waits for them, and re-layouts: 1.57 us -> none
    convert_element_type x0 -> x1, other arithmetic: none -> 0.67 us  [shards(): return (-mixing * total).astype(orbitals.dtype)]
where the time goes in v2:
time: 18.6 us; the launch traced here: 18.5 us
  Pallas kernels  17.8 us (96%)
  other arithmetic  0.67 us (4%)
    pallas_call x1, Pallas kernels, shards(): pl.pallas_call(functools.partial(kernel, blks), out_shape=jax.ShapeDtypeS...  17.8 us
    convert_element_type x1, other arithmetic, shards(): return (-mixing * total).astype(orbitals.dtype)  0.67 us

profile of v2, /device:TPU:0, one launch (start us, length us, event | category | flops | bytes accessed | tf_op | source)
XLA Modules:
  0.0 18.5 jit_solution(9755587454191700693)
XLA Ops:
  0.0 17.8 %shard_map.73 = f32[1,40,1600]{2,1,0:T(8,128)S(1)} custom-call(bf16[1,40,1600]{2,1,0:T(8,128)(2,1)} %orb_hbm.1, bf16[1,40,1600]{2,1,0:T(8,128)(2,1)} %resp_hbm.1, s32[1,4]{1,0:T(1,128)} %mask_hbm.1, f32[40,1600]{1,0:T(8,128)} %constant.11.clone.zt_hbm, f32[20,2,1600]{2,1,0:T(2,128)} %constant.12.clone.yt_hbm, bf16[80,80]{1,0:T(8,128)(2,1)} %constant.10.clone.left_hbm, ...), custom_call_target="tpu_custom_call" | custom-call | tf_op jit(solution)/shard_map/pallas_call | solution.py:219
  17.8 0.7 %multiply_convert_fusion = bf16[1,40,1600]{2,1,0:T(8,128)(2,1)} fusion(f32[1,40,1600]{2,1,0:T(8,128)S(1)} %shard_map.73), kind=kLoop, calls=%fused_computation | loop fusion | flops 128000 | bytes 384000 | tf_op jit(solution)/shard_map/convert_element_type | solution.py:250

commit v3 on v2

--- a/solution.py
+++ b/solution.py
@@ -39,7 +39,7 @@
 BACK = True
 PRIOR = True
 MATE = True
-chunk_in = 512
+chunk_in = 256
 chunk_out = 512
 
 

time: 18.6 us -> 18.6 us (level)
  no operation moved by 1% of the time
where the time goes in v3:
time: 18.6 us; the launch traced here: 18.4 us
  Pallas kernels  17.8 us (96%)
  other arithmetic  0.67 us (4%)
    pallas_call x1, Pallas kernels, shards(): pl.pallas_call(functools.partial(kernel, blks), out_shape=jax.ShapeDtypeS...  17.8 us
    convert_element_type x1, other arithmetic, shards(): return (-mixing * total).astype(orbitals.dtype)  0.67 us

profile of v3, /device:TPU:0, one launch (start us, length us, event | category | flops | bytes accessed | tf_op | source)
XLA Modules:
  0.0 18.4 jit_solution(1933910537557325602)
XLA Ops:
  0.0 17.8 %shard_map.73 = f32[1,40,1600]{2,1,0:T(8,128)S(1)} custom-call(bf16[1,40,1600]{2,1,0:T(8,128)(2,1)} %orb_hbm.1, bf16[1,40,1600]{2,1,0:T(8,128)(2,1)} %resp_hbm.1, s32[1,4]{1,0:T(1,128)} %mask_hbm.1, f32[40,1600]{1,0:T(8,128)} %constant.11.clone.zt_hbm, f32[20,2,1600]{2,1,0:T(2,128)} %constant.12.clone.yt_hbm, bf16[80,80]{1,0:T(8,128)(2,1)} %constant.10.clone.left_hbm, ...), custom_call_target="tpu_custom_call" | custom-call | tf_op jit(solution)/shard_map/pallas_call | solution.py:219
  17.8 0.7 %multiply_convert_fusion = bf16[1,40,1600]{2,1,0:T(8,128)(2,1)} fusion(f32[1,40,1600]{2,1,0:T(8,128)S(1)} %shard_map.73), kind=kLoop, calls=%fused_computation | loop fusion | flops 128000 | bytes 384000 | tf_op jit(solution)/shard_map/convert_element_type | solution.py:250

commit v4 on v3

--- a/solution.py
+++ b/solution.py
@@ -63,7 +63,7 @@
     to_prev = (grp, lax.rem(blk + blks - 1, blks), cross)
 
     barrier = pltpu.get_barrier_semaphore()
-    for device in (to_mate, to_prev):
+    for device in (to_prev, to_mate):
         pl.semaphore_signal(barrier, inc=1, device_id=device, device_id_type=MESH)
 
     own = [

time: 18.6 us -> 18.6 us (level)
  no operation moved by 1% of the time
where the time goes in v4:
time: 18.6 us; the launch traced here: 18.4 us
  Pallas kernels  17.8 us (96%)
  other arithmetic  0.67 us (4%)
    pallas_call x1, Pallas kernels, shards(): pl.pallas_call(functools.partial(kernel, blks), out_shape=jax.ShapeDtypeS...  17.8 us
    convert_element_type x1, other arithmetic, shards(): return (-mixing * total).astype(orbitals.dtype)  0.67 us

profile of v4, /device:TPU:0, one launch (start us, length us, event | category | flops | bytes accessed | tf_op | source)
XLA Modules:
  0.0 18.4 jit_solution(5878216232168290773)
XLA Ops:
  0.0 17.8 %shard_map.73 = f32[1,40,1600]{2,1,0:T(8,128)S(1)} custom-call(bf16[1,40,1600]{2,1,0:T(8,128)(2,1)} %orb_hbm.1, bf16[1,40,1600]{2,1,0:T(8,128)(2,1)} %resp_hbm.1, s32[1,4]{1,0:T(1,128)} %mask_hbm.1, f32[40,1600]{1,0:T(8,128)} %constant.11.clone.zt_hbm, f32[20,2,1600]{2,1,0:T(2,128)} %constant.12.clone.yt_hbm, bf16[80,80]{1,0:T(8,128)(2,1)} %constant.10.clone.left_hbm, ...), custom_call_target="tpu_custom_call" | custom-call | tf_op jit(solution)/shard_map/pallas_call | solution.py:219
  17.8 0.7 %multiply_convert_fusion = bf16[1,40,1600]{2,1,0:T(8,128)(2,1)} fusion(f32[1,40,1600]{2,1,0:T(8,128)S(1)} %shard_map.73), kind=kLoop, calls=%fused_computation | loop fusion | flops 128000 | bytes 384000 | tf_op jit(solution)/shard_map/convert_element_type | solution.py:250
